TPU v7x, 32 devices: a whole 2x2x4 slice. The times are simulated.
32 devices in a mesh: row: 4 (over z), col: 2 (over x), pole: 4 (over y, core).
Axes of the slice: x: 2, y: 2, z: 4, core: 2. Of those that a mesh axis runs over, the one named last changes fastest.
Arguments:
- window: bfloat16 [4, 8192, 8192], P('pole', 'col', 'row'), may hold values from -6 to 6
- panels: bfloat16 [4, 2, 8192, 256], P('pole', 'col', 'row'), may hold values from -0.0625 to 0.0625
- row_map: int32 [3, 8192], P(None, 'row'), may hold values from 0 to 8191, as said below
- panel_root: int32 [4, 3], P('pole'), may hold values from 0 to 1
- upper_blocks: bfloat16 [4, 3, 256, 256], P('pole', None, 'row'), may hold values from -0.375 to 0.375
- diag_inverse: float32 [4, 3, 256, 256], P('pole', None, 'row'), may hold values from -6 to 6
- weights: float32 [4], replicated, may hold values from 0.25 to 1
- pole_order: int32 [4], P('pole'), may hold values from 0 to 3, each once
Outputs:
- inv_columns: float32 [3, 2, 4096, 256], P(None, 'col', ('row', 'pole'))
- inv_diag: float32 [3, 256, 256], P(None, ('row', 'pole'))
Inputs may be any that keep to these rules, and one draw needn't show every extreme that they name: row_map[k] permutes the positions inside each aligned group of 1024 consecutive positions. `pole_order`: each of the 4 poles appears once.
All inputs are finite; a program needn't handle non-finite values.
Results may differ from a plain program's by a relative error of at most 0.0003.
Values may be sent and summed in bfloat16 or wider, within the bound.
A program may use at most 128 MiB of HBM per device.

v0:
```python
import jax
import jax.numpy as jnp
from jax import lax
from jax.sharding import PartitionSpec as P

NS = 3


def precise(left, right):
    return jnp.dot(left, right, precision=lax.Precision.HIGHEST, preferred_element_type=jnp.float32)


def pair_index(current, earlier):
    return current * (current - 1) // 2 + earlier


def inverse_block(diagonals, crossed, first, second):
    if first == second:
        return diagonals[first]
    if first < second:
        return crossed[first, second]
    return crossed[second, first].T


def window_term(window_block, aligned):
    return jnp.dot(window_block, aligned, preferred_element_type=jnp.float32)


def shards(window, panels, row_map, panel_root, upper_blocks, diag_inverse, weights, pole_order):
    window_block = window[0]
    panel_slab = panels[0, 0]
    pole_roots = panel_root[0]
    band_rows = panel_slab.shape[0]
    group_rows = window_block.shape[0] // lax.axis_size("row")
    row_index = lax.axis_index("row")
    col_index = lax.axis_index("col")
    gathered_upper, gathered_inverse = (
        lax.all_gather(upper_blocks.astype(jnp.float32), "row", axis=2, tiled=True).astype(
            upper_blocks.dtype
        ),
        lax.all_gather(diag_inverse, "row", axis=2, tiled=True),
    )
    factors = gathered_upper[0].astype(jnp.float32)
    inverses = gathered_inverse[0]
    share_rows = inverses.shape[1] // lax.axis_size("row")
    slot_panels = lax.all_gather(panels, "col", axis=1, tiled=True)[0]
    pole_weight = jnp.sum(jnp.where(jnp.arange(weights.shape[0]) == pole_order[0], weights, 0.0))
    columns = []
    diagonals = []
    crossed = {}
    for current in range(NS):
        received = lax.dynamic_index_in_dim(slot_panels, pole_roots[current], 0, keepdims=False)
        aligned = jnp.take(received, row_map[current] - row_index * band_rows, axis=0)
        own_rows = lax.dynamic_slice_in_dim(aligned, col_index * group_rows, group_rows, 0).astype(
            jnp.float32
        )
        partials = [precise(columns[earlier].T, own_rows) for earlier in range(current)]
        window_sum = lax.psum_scatter(
            window_term(window_block, aligned), "row", scatter_dimension=0, tiled=True
        )
        y_window = window_sum
        for earlier in range(current):
            y_window = y_window + precise(columns[earlier], factors[pair_index(current, earlier)])
        congruence = precise(own_rows.T, y_window)
        stacked = lax.psum(jnp.stack(partials + [congruence]), ("row", "col"))
        summed_cross = stacked[:current]
        summed_own = stacked[current]
        y_blocks = []
        for earlier in range(current):
            block_sum = summed_cross[earlier]
            for other_node in range(current):
                block_sum = block_sum + precise(
                    inverse_block(diagonals, crossed, earlier, other_node),
                    factors[pair_index(current, other_node)],
                )
            y_blocks.append(block_sum)
        diagonal = inverses[current] + summed_own
        for earlier in range(current):
            diagonal = diagonal + precise(
                factors[pair_index(current, earlier)].T, y_blocks[earlier]
            )
            crossed[earlier, current] = -y_blocks[earlier]
        columns.append(-y_window)
        diagonals.append(diagonal)
    column_terms = jnp.stack(columns) * pole_weight
    diagonal_terms = (
        jnp.stack(
            [
                lax.dynamic_slice_in_dim(diagonal, row_index * share_rows, share_rows, 0)
                for diagonal in diagonals
            ]
        )
        * pole_weight
    )
    summed_columns, summed_diagonals = (
        lax.psum_scatter(column_terms, "pole", scatter_dimension=1, tiled=True),
        lax.psum_scatter(diagonal_terms, "pole", scatter_dimension=1, tiled=True),
    )
    return (summed_columns[:, None], summed_diagonals)


def solution(mesh):
    return jax.shard_map(
        shards,
        mesh=mesh,
        in_specs=(
            P("pole", "col", "row"),
            P("pole", "col", "row", None),
            P(None, "row"),
            P("pole", None),
            P("pole", None, "row", None),
            P("pole", None, "row", None),
            P(),
            P("pole"),
        ),
        out_specs=(P(None, "col", ("row", "pole"), None), P(None, ("row", "pole"), None)),
        check_vma=False,
    )
```

profile of v0, /device:TPU:0, one launch (start us, length us, event | category | flops | bytes accessed | tf_op | source)
XLA Modules:
  0.0 490.8 jit_solution(11846383781759528025)
XLA Ops:
  7.2 0.0 all-gather.2.cloned.1.call-start
  7.2 0.7 all-gather.2.cloned.1.call-update
  7.9 0.0 reduce-scatter.6.cloned.1.call-start
  7.9 1.4 fusion.45
  15.1 0.9 slice_subtract_fusion.1
  16.0 29.3 %all-gather.2.cloned.1.call-done = bf16[1,2,2048,256]{3,2,0,1:T(8,128)(2,1)} async-done(((bf16[1,1,2048,256]{3,2,0,1:T(8,128)(2,1)}), bf16[1,2,2048,256]{3,2,0,1:T(8,128)(2,1)}) %all-gather.2.cloned.1.call-update) | async-done | bytes 2097168 | tf_op jit(solution)/shard_map/all_gather | solution.py:46
  45.4 2.2 dynamic-slice_bitcast_fusion.1
  47.6 9.0 %gather_fusion = bf16[2048,256]{1,0:T(8,128)(2,1)} fusion(bf16[2048,256]{1,0:T(8,128)(2,1)S(1)} %get-tuple-element.12, s32[2048]{0:T(1024)S(1)} %fusion.35), kind=kCustom, calls=%fused_computation.clone | custom fusion | bytes 2105344 | tf_op jit(solution)/shard_map/jit(_take)/gather | solution.py:53
  56.6 1.5 broadcast_select_fusion.2
  58.1 10.5 %fusion.6 = f32[4096,256]{0,1:T(8,128)} fusion(bf16[2048,256]{1,0:T(8,128)(2,1)S(1)} %broadcast_select_fusion.2, bf16[1,4096,2048]{2,1,0:T(8,128)(2,1)} %param.10), kind=kOutput, calls=%fused_computation.9 | convolution fusion | flops 4294967296 | bytes 22020096 | tf_op jit(solution)/shard_map/dot_general | solution.py:26
  68.6 0.0 reduce-scatter.6.cloned.1.call-update
  68.6 0.0 reduce-scatter.8.cloned.1.call-start
  68.7 7.5 %gather_fusion.1 = bf16[2048,256]{1,0:T(8,128)(2,1)S(1)} fusion(bf16[2048,256]{1,0:T(8,128)(2,1)S(1)} %get-tuple-element.10, s32[2048]{0:T(1024)S(1)} %fusion.36), kind=kCustom, calls=%fused_computation.1.clone | custom fusion | bytes 2105344 | tf_op jit(solution)/shard_map/jit(_take)/gather | solution.py:53
  76.2 0.4 broadcast_select_fusion.1
  76.7 10.6 %fusion.9 = f32[4096,256]{0,1:T(8,128)} fusion(bf16[2048,256]{1,0:T(8,128)(2,1)S(1)} %broadcast_select_fusion.1, bf16[1,4096,2048]{2,1,0:T(8,128)(2,1)} %param.10), kind=kOutput, calls=%fused_computation.10 | convolution fusion | flops 4294967296 | bytes 22020096 | tf_op jit(solution)/shard_map/dot_general | solution.py:26
  87.3 0.0 reduce-scatter.8.cloned.1.call-update
  87.3 0.0 reduce-scatter.10.cloned.1.call-start
  87.4 7.5 %gather_fusion.2 = bf16[2048,256]{1,0:T(8,128)(2,1)S(1)} fusion(bf16[2048,256]{1,0:T(8,128)(2,1)S(1)} %get-tuple-element.11, s32[2048]{0:T(1024)S(1)} %fusion.37), kind=kCustom, calls=%fused_computation.2.clone | custom fusion | bytes 2105344 | tf_op jit(solution)/shard_map/jit(_take)/gather | solution.py:53
  94.9 0.4 broadcast_select_fusion
  95.3 10.6 %fusion.12 = f32[4096,256]{0,1:T(8,128)} fusion(bf16[2048,256]{1,0:T(8,128)(2,1)S(1)} %broadcast_select_fusion, bf16[1,4096,2048]{2,1,0:T(8,128)(2,1)} %param.10), kind=kOutput, calls=%fused_computation.11 | convolution fusion | flops 4294967296 | bytes 22020096 | tf_op jit(solution)/shard_map/dot_general | solution.py:26
  105.9 0.0 reduce-scatter.10.cloned.1.call-update
  105.9 0.0 all-reduce.3.cloned.1.call-start
  106.0 0.8 copy-done.11
  106.8 20.3 %all_gather.10 = bf16[1,3,256,256]{3,2,1,0:T(8,128)(2,1)S(1)} all-gather(bf16[1,3,64,256]{3,2,1,0:T(8,128)(2,1)S(1)} %copy-done.11), channel_id=1, replica_groups=mesh['row'=4,'col'=2,'pole'=4] {'row'}, dimensions={2}, use_global_device_ids=true | all-gather | bytes 491520 | tf_op jit(solution)/shard_map/all_gather | solution.py:38
  127.2 24.6 %reduce-scatter.6.cloned.1.call-done = f32[1024,256]{0,1:T(8,128)} async-done(((f32[4096,256]{0,1:T(8,128)}), f32[1024,256]{0,1:T(8,128)}) %reduce-scatter.6.cloned.1.call-update) | async-done | bytes 1048592 | tf_op jit(solution)/shard_map/reduce_scatter | solution.py:58
  151.8 79.5 %reduce-scatter.8.cloned.1.call-done = f32[1024,256]{0,1:T(8,128)} async-done(((f32[4096,256]{0,1:T(8,128)}), f32[1024,256]{0,1:T(8,128)}) %reduce-scatter.8.cloned.1.call-update) | async-done | bytes 1048592 | tf_op jit(solution)/shard_map/reduce_scatter | solution.py:58
  231.3 2.2 convolution_add_fusion.2
  233.6 2.5 convolution_bitcast_fusion.6
  236.1 1.3 convolution_bitcast_fusion.4
  237.4 73.4 %reduce-scatter.10.cloned.1.call-done = f32[1024,256]{0,1:T(8,128)} async-done(((f32[4096,256]{0,1:T(8,128)}), f32[1024,256]{0,1:T(8,128)}) %reduce-scatter.10.cloned.1.call-update) | async-done | bytes 1048592 | tf_op jit(solution)/shard_map/reduce_scatter | solution.py:58
  310.8 2.1 convolution_add_fusion.1
  312.9 0.7 convolution_add_fusion
  313.7 0.8 convolution_bitcast_fusion.3
  314.4 0.6 convolution_bitcast_fusion.7
  315.1 0.8 pad_maximum_fusion.1
  315.9 0.6 convolution_bitcast_fusion.5
  316.6 0.9 pad_maximum_fusion
  317.5 1.5 convolution_bitcast_fusion.8
  319.0 0.0 all-reduce.3.cloned.1.call-update
  319.0 0.0 reduce-scatter.12.cloned.1.call-start
  319.7 0.6 fusion.44
  320.3 0.1 negate_bitcast_fusion.2
  320.4 0.2 negate_bitcast_fusion
  320.6 0.0 copy-start.10
  320.6 2.6 maximum_multiply_fusion
  323.2 0.0 reduce-scatter.12.cloned.1.call-update
  323.2 0.0 reduce-scatter.14.cloned.1.call-start
  323.3 31.1 %all_gather.11 = f32[1,3,256,256]{3,2,1,0:T(8,128)S(1)} all-gather(f32[1,3,64,256]{3,2,1,0:T(8,128)S(1)} %copy-done.10), channel_id=1, replica_groups=mesh['row'=4,'col'=2,'pole'=4] {'row'}, dimensions={2}, use_global_device_ids=true | all-gather | bytes 983040 | tf_op jit(solution)/shard_map/all_gather | solution.py:41
  354.4 67.3 %all-reduce.3.cloned.1.call-done = (f32[3,256,256]{2,1,0:T(8,128)}, f32[2,256,256]{2,1,0:T(8,128)}, f32[1,256,256]{2,1,0:T(8,128)}) async-done(((f32[3,256,256]{2,1,0:T(8,128)}, f32[2,256,256]{2,1,0:T(8,128)}, f32[1,256,256]{2,1,0:T(8,128)}), (f32[3,256,256]{2,1,0:T(8,128)}, f32[2,256,256]{2,1,0:T(8,128)}, f32[1,256,256]{2,1,0:T(8,128)})) %all-reduce.3.cloned.1.call-update) | async-done | bytes 1572880 | tf_op jit(solution)/shard_map/psum | solution.py:65
  421.8 0.9 fusion.34
  422.7 1.0 slice_bitcast_fusion.2
  423.6 1.3 convolution_add_fusion.6
  424.9 1.3 convolution_add_fusion.7
  426.3 0.3 convolution_add_fusion.5
  426.5 0.3 convolution_bitcast_fusion.1
  426.9 1.3 convolution_add_fusion.4
  428.2 0.3 fusion.15
  428.5 0.3 convolution_add_fusion.3
  428.8 0.3 convolution_bitcast_fusion
  429.2 1.3 maximum_multiply_fusion.1
  430.4 0.0 reduce-scatter.14.cloned.1.call-update
  430.5 30.6 %reduce-scatter.12.cloned.1.call-done = f32[3,256,256]{1,2,0:T(8,128)} async-done(((f32[3,1024,256]{1,2,0:T(8,128)}), f32[3,256,256]{1,2,0:T(8,128)}) %reduce-scatter.12.cloned.1.call-update) | async-done | bytes 786448 | tf_op jit(solution)/shard_map/reduce_scatter | solution.py:96
  461.1 2.3 copy.18
  463.4 20.6 %reduce-scatter.14.cloned.1.call-done = f32[3,16,256]{2,1,0:T(8,128)} async-done(((f32[3,64,256]{2,1,0:T(8,128)}), f32[3,16,256]{2,1,0:T(8,128)}) %reduce-scatter.14.cloned.1.call-update) | async-done | bytes 49168 | tf_op jit(solution)/shard_map/reduce_scatter | solution.py:97
  (32 shorter events, 0.2 us)
Async XLA Ops:
  7.2 38.2 %all-gather.2.cloned.1.call-start = ((), (), s32[]{:S(2)}) async-start(), calls=%async_computation.5 | async-start | bytes 3145728 | tf_op jit(solution)/shard_map/all_gather | solution.py:46
  7.9 143.9 %reduce-scatter.6.cloned.1.call-start = ((), (), s32[]{:S(2)}) async-start(), calls=%async_computation.6 | async-start | bytes 5242880 | tf_op jit(solution)/shard_map/reduce_scatter | solution.py:58
  58.1 10.5 %copy-start.5 = (bf16[2048,256]{1,0:T(8,128)(2,1)}, bf16[2048,256]{1,0:T(8,128)(2,1)S(1)}, u32[]{:S(2)}) copy-start(bf16[2048,256]{1,0:T(8,128)(2,1)S(1)} %broadcast_select_fusion.2) | copy-start | bytes 3145732
  68.6 162.7 %reduce-scatter.8.cloned.1.call-start = ((), (), s32[]{:S(2)}) async-start(), calls=%async_computation.7 | async-start | bytes 5242880 | tf_op jit(solution)/shard_map/reduce_scatter | solution.py:58
  76.7 10.6 %copy-start.3 = (bf16[2048,256]{1,0:T(8,128)(2,1)}, bf16[2048,256]{1,0:T(8,128)(2,1)S(1)}, u32[]{:S(2)}) copy-start(bf16[2048,256]{1,0:T(8,128)(2,1)S(1)} %broadcast_select_fusion.1) | copy-start | bytes 3145732
  87.3 223.5 %reduce-scatter.10.cloned.1.call-start = ((), (), s32[]{:S(2)}) async-start(), calls=%async_computation.8 | async-start | bytes 5242880 | tf_op jit(solution)/shard_map/reduce_scatter | solution.py:58
  95.3 140.8 %copy-start.1 = (bf16[2048,256]{1,0:T(8,128)(2,1)}, bf16[2048,256]{1,0:T(8,128)(2,1)S(1)}, u32[]{:S(2)}) copy-start(bf16[2048,256]{1,0:T(8,128)(2,1)S(1)} %broadcast_select_fusion) | copy-start | bytes 3145732
  105.9 0.9 copy-start.11
  105.9 315.8 %all-reduce.3.cloned.1.call-start = ((), (), s32[]{:S(2)}) async-start(), calls=%async_computation.11 | async-start | bytes 3145728 | tf_op jit(solution)/shard_map/psum | solution.py:65
  151.8 159.0 %copy-start = (f32[1024,256]{0,1:T(8,128)S(1)}, f32[1024,256]{0,1:T(8,128)}, u32[]{:S(2)}) copy-start(f32[1024,256]{0,1:T(8,128)} %reduce-scatter.6.cloned.1.call-done) | copy-start | bytes 3145732
  310.8 2.8 copy-start.2
  310.8 3.6 copy-start.4
  312.9 2.2 copy-start.8
  312.9 3.7 copy-start.7
  313.6 3.9 copy-start.6
  315.1 4.6 copy-start.12
  319.0 142.1 %reduce-scatter.12.cloned.1.call-start = ((), (), s32[]{:S(2)}) async-start(), calls=%async_computation.9 | async-start | bytes 3932160 | tf_op jit(solution)/shard_map/reduce_scatter | solution.py:96
  320.6 2.6 copy-start.10
  323.2 160.7 %reduce-scatter.14.cloned.1.call-start = ((), (), s32[]{:S(2)}) async-start(), calls=%async_computation.10 | async-start | bytes 245760 | tf_op jit(solution)/shard_map/reduce_scatter | solution.py:97
  421.8 6.5 %copy-start.9 = (f32[2,256,256]{2,1,0:T(8,128)S(1)}, f32[2,256,256]{2,1,0:T(8,128)}, u32[]{:S(2)}) copy-start(f32[2,256,256]{2,1,0:T(8,128)} %get-tuple-element.8) | copy-start | bytes 1572868
Sparse Core Ops, SparseCore 0:
  9.5 35.8 all-gather.1
  68.8 82.9 reduce-scatter.5
  154.1 77.2 reduce-scatter.7
  233.5 77.2 reduce-scatter.9
  319.2 102.5 all-reduce.2
  424.1 36.9 reduce-scatter.11
  464.1 19.7 reduce-scatter.13
where the time goes:
time: 491 us
  waiting for transfers between devices  326 us (66%)
  blocking collectives  51.5 us (10%)
  matrix products  49.5 us (10%)
  local copies, waits for them, and re-layouts  31.8 us (6%)
  between operations  20.9 us (4%)
  other arithmetic  10.7 us (2%)
    reduce_scatter x3, waiting for transfers between devices, shards(): lax.psum_scatter(window_term(window_block, aligned), 'row', scatter_dimen...  178 us
    psum x1, waiting for transfers between devices, shards(): stacked = lax.psum(jnp.stack(partials + [congruence]), ('row', 'col'))  67.3 us
    dot_general x3, matrix products, window_term(): return jnp.dot(window_block, aligned, preferred_element_type=jnp.float32)  31.7 us
    all_gather x1, blocking collectives, shards(): lax.all_gather(diag_inverse, 'row', axis=2, tiled=True)  31.1 us
    reduce_scatter x1, waiting for transfers between devices, shards(): lax.psum_scatter(column_terms, 'pole', scatter_dimension=1, tiled=True)  30.6 us
    all_gather x1, waiting for transfers between devices, shards(): slot_panels = lax.all_gather(panels, 'col', axis=1, tiled=True)[0]  29.3 us
    gather x3, local copies, waits for them, and re-layouts, shards(): jnp.take(received, row_map[current] - row_index * band_rows, axis=0)  24 us
    reduce_scatter x1, waiting for transfers between devices, shards(): lax.psum_scatter(diagonal_terms, 'pole', scatter_dimension=1, tiled=True)  20.6 us
  transfers between devices with their start and end apart: 7, of which 7 were waited for; matrix products, arithmetic and copies ran while one was open for 12% of the time, Pallas kernels for 0%

commit v1 on v0

--- a/solution.py
+++ b/solution.py
@@ -62,7 +62,9 @@
         for earlier in range(current):
             y_window = y_window + precise(columns[earlier], factors[pair_index(current, earlier)])
         congruence = precise(own_rows.T, y_window)
-        stacked = lax.psum(jnp.stack(partials + [congruence]), ("row", "col"))
+        stacked = jnp.sum(
+            lax.all_gather(jnp.stack(partials + [congruence]), ("row", "col")), axis=0
+        )
         summed_cross = stacked[:current]
         summed_own = stacked[current]
         y_blocks = []

time: 491 us -> 607 us (1.24)
  waiting for transfers between devices: 326 us -> 445 us
  blocking collectives: 51.5 us -> 42.6 us
  other arithmetic: 10.7 us -> 18.6 us
    all_gather x0 -> x3, waiting for transfers between devices: none -> 189 us  [shards(): lax.all_gather(jnp.stack(partials + [congruence]), ('row', 'col'))]
    psum x1 -> x0, waiting for transfers between devices: 67.3 us -> none  [shards(): stacked = lax.psum(jnp.stack(partials + [congruence]), ('row', 'col'))]
    reduce_sum x0 -> x3, other arithmetic: none -> 7.56 us  [shards(): jnp.sum(lax.all_gather(jnp.stack(partials + [congruence]), ('row', 'col')...]
    all_gather x1, blocking collectives: 31.1 us -> 23.8 us  [shards(): lax.all_gather(diag_inverse, 'row', axis=2, tiled=True)]
  transfers between devices with their start and end apart: 7 -> 9, of which waited for: 7 -> 9; matrix products, arithmetic and copies ran while one was open for 12% -> 12% of each run, Pallas kernels for 0% -> 0%
where the time goes in v1:
time: 607 us; the launch traced here: 606 us
  waiting for transfers between devices  445 us (73%)
  matrix products  47 us (8%)
  blocking collectives  42.6 us (7%)
  local copies, waits for them, and re-layouts  31.5 us (5%)
  between operations  20.8 us (3%)
  other arithmetic  18.6 us (3%)
    all_gather x3, waiting for transfers between devices, shards(): lax.all_gather(jnp.stack(partials + [congruence]), ('row', 'col'))  189 us
    reduce_scatter x3, waiting for transfers between devices, shards(): lax.psum_scatter(window_term(window_block, aligned), 'row', scatter_dimen...  174 us
    reduce_scatter x1, waiting for transfers between devices, shards(): lax.psum_scatter(column_terms, 'pole', scatter_dimension=1, tiled=True)  31.9 us
    dot_general x3, matrix products, window_term(): return jnp.dot(window_block, aligned, preferred_element_type=jnp.float32)  31.3 us
    all_gather x1, waiting for transfers between devices, shards(): slot_panels = lax.all_gather(panels, 'col', axis=1, tiled=True)[0]  29.2 us
    gather x3, local copies, waits for them, and re-layouts, shards(): jnp.take(received, row_map[current] - row_index * band_rows, axis=0)  25.5 us
    all_gather x1, blocking collectives, shards(): lax.all_gather(diag_inverse, 'row', axis=2, tiled=True)  23.8 us
    reduce_scatter x1, waiting for transfers between devices, shards(): lax.psum_scatter(diagonal_terms, 'pole', scatter_dimension=1, tiled=True)  20.6 us
  transfers between devices with their start and end apart: 9, of which 9 were waited for; matrix products, arithmetic and copies ran while one was open for 12% of the time, Pallas kernels for 0%

profile of v1, /device:TPU:0, one launch (start us, length us, event | category | flops | bytes accessed | tf_op | source)
XLA Modules:
  0.0 606.3 jit_solution(17494644715491442112)
XLA Ops:
  7.2 0.0 all-gather.8.cloned.1.call-start
  7.2 0.7 all-gather.8.cloned.1.call-update
  7.9 0.0 reduce-scatter.6.cloned.1.call-start
  7.9 1.4 fusion.46
  15.3 0.9 slice_subtract_fusion.1
  16.2 29.2 %all-gather.8.cloned.1.call-done = bf16[1,2,2048,256]{3,2,0,1:T(8,128)(2,1)} async-done(((bf16[1,1,2048,256]{3,2,0,1:T(8,128)(2,1)}), bf16[1,2,2048,256]{3,2,0,1:T(8,128)(2,1)}) %all-gather.8.cloned.1.call-update) | async-done | bytes 2097168 | tf_op jit(solution)/shard_map/all_gather | solution.py:46
  45.4 2.2 dynamic-slice_bitcast_fusion.1
  47.6 9.0 %gather_fusion = bf16[2048,256]{1,0:T(8,128)(2,1)} fusion(bf16[2048,256]{1,0:T(8,128)(2,1)S(1)} %get-tuple-element.9, s32[2048]{0:T(1024)S(1)} %fusion.36), kind=kCustom, calls=%fused_computation.clone | custom fusion | bytes 2105344 | tf_op jit(solution)/shard_map/jit(_take)/gather | solution.py:53
  56.6 1.5 broadcast_select_fusion.2
  58.1 10.6 %fusion.6 = f32[4096,256]{0,1:T(8,128)} fusion(bf16[2048,256]{1,0:T(8,128)(2,1)S(1)} %broadcast_select_fusion.2, bf16[1,4096,2048]{2,1,0:T(8,128)(2,1)} %param.10), kind=kOutput, calls=%fused_computation.9 | convolution fusion | flops 4294967296 | bytes 22020096 | tf_op jit(solution)/shard_map/dot_general | solution.py:26
  68.6 0.0 reduce-scatter.6.cloned.1.call-update
  68.7 0.0 reduce-scatter.8.cloned.1.call-start
  68.7 9.0 %gather_fusion.1 = bf16[2048,256]{1,0:T(8,128)(2,1)} fusion(bf16[2048,256]{1,0:T(8,128)(2,1)S(1)} %get-tuple-element.7, s32[2048]{0:T(1024)S(1)} %fusion.37), kind=kCustom, calls=%fused_computation.1.clone | custom fusion | bytes 2105344 | tf_op jit(solution)/shard_map/jit(_take)/gather | solution.py:53
  77.7 1.5 broadcast_select_fusion.1
  79.2 10.2 %fusion.9 = f32[4096,256]{0,1:T(8,128)} fusion(bf16[2048,256]{1,0:T(8,128)(2,1)S(1)} %broadcast_select_fusion.1, bf16[1,4096,2048]{2,1,0:T(8,128)(2,1)} %param.10), kind=kOutput, calls=%fused_computation.10 | convolution fusion | flops 4294967296 | bytes 22020096 | tf_op jit(solution)/shard_map/dot_general | solution.py:26
  89.5 0.0 reduce-scatter.10.cloned.1.call-start
  89.6 7.5 %gather_fusion.2 = bf16[2048,256]{1,0:T(8,128)(2,1)S(1)} fusion(bf16[2048,256]{1,0:T(8,128)(2,1)S(1)} %get-tuple-element.8, s32[2048]{0:T(1024)S(1)} %fusion.38), kind=kCustom, calls=%fused_computation.2.clone | custom fusion | bytes 2105344 | tf_op jit(solution)/shard_map/jit(_take)/gather | solution.py:53
  97.1 0.4 broadcast_select_fusion
  97.5 10.5 %fusion.12 = f32[4096,256]{0,1:T(8,128)} fusion(bf16[2048,256]{1,0:T(8,128)(2,1)S(1)} %broadcast_select_fusion, bf16[1,4096,2048]{2,1,0:T(8,128)(2,1)} %param.10), kind=kOutput, calls=%fused_computation.11 | convolution fusion | flops 4294967296 | bytes 22020096 | tf_op jit(solution)/shard_map/dot_general | solution.py:26
  108.1 0.0 reduce-scatter.10.cloned.1.call-update
  108.1 0.0 all-gather.10.cloned.1.call-start
  108.2 37.3 %reduce-scatter.6.cloned.1.call-done = f32[1024,256]{0,1:T(8,128)} async-done(((f32[4096,256]{0,1:T(8,128)}), f32[1024,256]{0,1:T(8,128)}) %reduce-scatter.6.cloned.1.call-update) | async-done | bytes 1048592 | tf_op jit(solution)/shard_map/reduce_scatter | solution.py:58
  145.5 2.8 fusion.22
  148.3 0.0 all-gather.12.cloned.1.call-start
  148.3 18.8 %all_gather.25 = bf16[1,3,256,256]{3,2,1,0:T(8,128)(2,1)S(1)} all-gather(bf16[1,3,64,256]{3,2,1,0:T(8,128)(2,1)} %param.14), channel_id=1, replica_groups=mesh['row'=4,'col'=2,'pole'=4] {'row'}, dimensions={2}, use_global_device_ids=true | all-gather | bytes 491520 | tf_op jit(solution)/shard_map/all_gather | solution.py:38
  167.1 61.9 %reduce-scatter.8.cloned.1.call-done = f32[1024,256]{0,1:T(8,128)} async-done(((f32[4096,256]{0,1:T(8,128)}), f32[1024,256]{0,1:T(8,128)}) %reduce-scatter.8.cloned.1.call-update) | async-done | bytes 1048592 | tf_op jit(solution)/shard_map/reduce_scatter | solution.py:58
  229.0 2.2 convolution_add_fusion.2
  231.3 0.8 convolution_bitcast_fusion.6
  232.1 0.6 convolution_bitcast_fusion.7
  232.7 0.9 pad_maximum_fusion.1
  233.6 0.0 all-gather.14.cloned.1.call-start
  233.6 75.0 %reduce-scatter.10.cloned.1.call-done = f32[1024,256]{0,1:T(8,128)} async-done(((f32[4096,256]{0,1:T(8,128)}), f32[1024,256]{0,1:T(8,128)}) %reduce-scatter.10.cloned.1.call-update) | async-done | bytes 1048592 | tf_op jit(solution)/shard_map/reduce_scatter | solution.py:58
  308.6 1.9 convolution_add_fusion.1
  310.6 0.7 convolution_add_fusion
  311.3 1.8 convolution_bitcast_fusion.3
  313.1 1.7 convolution_bitcast_fusion.4
  314.8 0.7 convolution_bitcast_fusion.5
  315.5 0.9 pad_maximum_fusion
  316.4 0.0 reduce-scatter.12.cloned.1.call-start
  317.2 0.6 fusion.45
  317.8 0.1 negate_bitcast_fusion
  317.9 0.1 negate_bitcast_fusion.1
  317.9 0.1 negate_bitcast_fusion.2
  318.0 2.7 maximum_multiply_fusion
  320.8 0.0 reduce-scatter.14.cloned.1.call-start
  320.8 23.8 %all_gather.26 = f32[1,3,256,256]{3,2,1,0:T(8,128)S(1)} all-gather(f32[1,3,64,256]{3,2,1,0:T(8,128)S(1)} %copy-done.5), channel_id=1, replica_groups=mesh['row'=4,'col'=2,'pole'=4] {'row'}, dimensions={2}, use_global_device_ids=true | all-gather | bytes 983040 | tf_op jit(solution)/shard_map/all_gather | solution.py:41
  344.7 20.4 %all-gather.10.cloned.1.call-done = f32[2048,256]{1,0:T(8,128)} async-done(((f32[256,256]{1,0:T(8,128)}), f32[2048,256]{1,0:T(8,128)}) %all-gather.10.cloned.1.call-update) | async-done | bytes 2097168 | tf_op jit(solution)/shard_map/all_gather | solution.py:66
  365.1 1.8 reduce.1
  366.8 71.5 %all-gather.12.cloned.1.call-done = f32[16,256,256]{2,1,0:T(8,128)} async-done(((f32[2,256,256]{2,1,0:T(8,128)}), f32[16,256,256]{2,1,0:T(8,128)}) %all-gather.12.cloned.1.call-update) | async-done | bytes 4194320 | tf_op jit(solution)/shard_map/all_gather | solution.py:66
  438.4 2.5 reduce_sum.38
  440.9 0.3 convolution_add_fusion.7
  441.2 0.3 fusion.15
  441.5 96.9 %all-gather.14.cloned.1.call-done = f32[24,256,256]{2,1,0:T(8,128)} async-done(((f32[3,256,256]{2,1,0:T(8,128)}), f32[24,256,256]{2,1,0:T(8,128)}) %all-gather.14.cloned.1.call-update) | async-done | bytes 6291472 | tf_op jit(solution)/shard_map/all_gather | solution.py:66
  538.4 3.3 reduce_sum.39
  541.7 0.3 convolution_add_fusion.6
  542.0 0.3 convolution_add_fusion.5
  542.3 0.3 convolution_bitcast_fusion.1
  542.6 0.4 convolution_add_fusion.4
  543.0 0.3 convolution_add_fusion.3
  543.3 0.3 convolution_bitcast_fusion
  543.6 1.3 maximum_multiply_fusion.1
  544.9 31.9 %reduce-scatter.12.cloned.1.call-done = f32[3,256,256]{1,2,0:T(8,128)} async-done(((f32[3,1024,256]{1,2,0:T(8,128)}), f32[3,256,256]{1,2,0:T(8,128)}) %reduce-scatter.12.cloned.1.call-update) | async-done | bytes 786448 | tf_op jit(solution)/shard_map/reduce_scatter | solution.py:98
  576.9 2.3 copy.18
  579.1 20.6 %reduce-scatter.14.cloned.1.call-done = f32[3,16,256]{2,1,0:T(8,128)} async-done(((f32[3,64,256]{2,1,0:T(8,128)}), f32[3,16,256]{2,1,0:T(8,128)}) %reduce-scatter.14.cloned.1.call-update) | async-done | bytes 49168 | tf_op jit(solution)/shard_map/reduce_scatter | solution.py:99
  (31 shorter events, 0.3 us)
Async XLA Ops:
  7.2 38.2 %all-gather.8.cloned.1.call-start = ((), (), s32[]{:S(2)}) async-start(), calls=%async_computation.5 | async-start | bytes 3145728 | tf_op jit(solution)/shard_map/all_gather | solution.py:46
  7.9 137.6 %reduce-scatter.6.cloned.1.call-start = ((), (), s32[]{:S(2)}) async-start(), calls=%async_computation.6 | async-start | bytes 5242880 | tf_op jit(solution)/shard_map/reduce_scatter | solution.py:58
  58.1 10.6 %copy-start.3 = (bf16[2048,256]{1,0:T(8,128)(2,1)}, bf16[2048,256]{1,0:T(8,128)(2,1)S(1)}, u32[]{:S(2)}) copy-start(bf16[2048,256]{1,0:T(8,128)(2,1)S(1)} %broadcast_select_fusion.2) | copy-start | bytes 3145732
  68.7 160.3 %reduce-scatter.8.cloned.1.call-start = ((), (), s32[]{:S(2)}) async-start(), calls=%async_computation.7 | async-start | bytes 5242880 | tf_op jit(solution)/shard_map/reduce_scatter | solution.py:58
  89.5 219.1 %reduce-scatter.10.cloned.1.call-start = ((), (), s32[]{:S(2)}) async-start(), calls=%async_computation.8 | async-start | bytes 5242880 | tf_op jit(solution)/shard_map/reduce_scatter | solution.py:58
  97.5 10.6 %copy-start.1 = (bf16[2048,256]{1,0:T(8,128)(2,1)}, bf16[2048,256]{1,0:T(8,128)(2,1)S(1)}, u32[]{:S(2)}) copy-start(bf16[2048,256]{1,0:T(8,128)(2,1)S(1)} %broadcast_select_fusion) | copy-start | bytes 3145732
  108.1 37.4 %copy-start.4 = (bf16[2048,256]{1,0:T(8,128)(2,1)S(1)}, bf16[2048,256]{1,0:T(8,128)(2,1)}, u32[]{:S(2)}) copy-start(bf16[2048,256]{1,0:T(8,128)(2,1)} %copy-done.3) | copy-start | bytes 3145732
  108.1 256.9 %all-gather.10.cloned.1.call-start = ((), (), s32[]{:S(2)}) async-start(), calls=%async_computation.11 | async-start | bytes 2359296 | tf_op jit(solution)/shard_map/all_gather | solution.py:66
  145.5 86.6 %copy-start = (f32[1024,256]{0,1:T(8,128)S(1)}, f32[1024,256]{0,1:T(8,128)}, u32[]{:S(2)}) copy-start(f32[1024,256]{0,1:T(8,128)} %reduce-scatter.6.cloned.1.call-done) | copy-start | bytes 3145732
  148.3 290.1 %all-gather.12.cloned.1.call-start = ((), (), s32[]{:S(2)}) async-start(), calls=%async_computation.12 | async-start | bytes 4718592 | tf_op jit(solution)/shard_map/all_gather | solution.py:66
  233.6 304.8 %all-gather.14.cloned.1.call-start = ((), (), s32[]{:S(2)}) async-start(), calls=%async_computation.13 | async-start | bytes 7077888 | tf_op jit(solution)/shard_map/all_gather | solution.py:66
  310.6 4.3 copy-start.2
  311.3 5.8 copy-start.6
  316.4 260.4 %reduce-scatter.12.cloned.1.call-start = ((), (), s32[]{:S(2)}) async-start(), calls=%async_computation.9 | async-start | bytes 3932160 | tf_op jit(solution)/shard_map/reduce_scatter | solution.py:98
  318.0 2.8 copy-start.5
  320.8 279.0 %reduce-scatter.14.cloned.1.call-start = ((), (), s32[]{:S(2)}) async-start(), calls=%async_computation.10 | async-start | bytes 245760 | tf_op jit(solution)/shard_map/reduce_scatter | solution.py:99
Sparse Core Ops, SparseCore 0:
  9.5 35.8 all-gather.7
  68.8 76.6 reduce-scatter.5
  147.7 81.2 reduce-scatter.7
  231.2 77.4 reduce-scatter.9
  310.6 54.4 all-gather.9
  367.0 71.3 all-gather.11
  441.1 97.2 all-gather.13
  540.9 35.8 reduce-scatter.11
  579.9 19.7 reduce-scatter.13
